TPU v7x, 32 devices: a whole 2x2x4 slice. The times are simulated.
32 devices in a mesh: blk: 8 (over z, x), rep: 4 (over y, core).
Axes of the slice: x: 2, y: 2, z: 4, core: 2. Of those that a mesh axis runs over, the one named last changes fastest.
Arguments:
- a_blocks: bfloat16 [24, 8, 6, 128, 128], P('blk', None, None, None, 'rep'), may hold values from -0.5 to 0.5
- a_cols: int32 [24, 8, 6], P('blk'), may hold values from 0 to 111, as said below
- b_blocks: bfloat16 [896, 4, 3, 128, 128], P('blk', 'rep'), may hold values from -6 to 6
- b_cols: int32 [896, 4, 3], P('blk', 'rep'), may hold values from 0 to 223, as said below
- c_cols: int32 [24, 4, 4], P(None, 'rep'), may hold values from 0 to 223, as said below
Outputs:
- c_blocks: float32 [24, 4, 4, 128, 128], P('blk', 'rep')
Inputs may be any that keep to these rules, and one draw needn't show every extreme that they name: `a_cols`: within each block row and panel the 6 entries are distinct. `b_cols`: within each block row and tile the 3 entries are distinct. `c_cols`: within each block row and tile the 4 entries are distinct.
All inputs are finite; a program needn't handle non-finite values.
Results may differ from a plain program's by a relative error of at most 0.0003.
Values may be sent and summed in bfloat16 or wider, within the bound.
No kernel may reach another device: no remote copies, remote signals or barrier semaphores. Data moves between devices by JAX's collectives and lax.ppermute only.
A program may use at most 128 MiB of HBM per device.

v0:
```python
import math
import jax
import jax.numpy as jnp
from jax import lax
from jax.sharding import PartitionSpec as P


def select_blocks(chosen, chosen_cols, wanted):
    hits = chosen_cols[..., :, None] == wanted
    total = None
    for slot_t in range(chosen.shape[-3]):
        term = jnp.where(
            hits[..., slot_t, :, None, None],
            chosen[..., slot_t, None, :, :],
            jnp.zeros((), chosen.dtype),
        )
        total = term if total is None else total + term
    return total


def term_maker(slab, slab_cols, local_b, local_bcols, pattern):
    total_rows = slab.shape[0]
    slots = slab.shape[2]
    width = slab.shape[3]
    slab = slab.reshape(total_rows, slots, width, width)
    slab_cols = slab_cols.reshape(total_rows, slots)

    def partial_term(start, count):
        group = math.gcd(count, 2)

        def one_group(index):
            first = index * group
            left = lax.dynamic_slice_in_dim(slab, first, group, 0)
            where_k = lax.dynamic_slice_in_dim(slab_cols, first, group, 0)
            wanted = lax.dynamic_slice_in_dim(pattern, first, group, 0)
            chosen = jnp.take(local_b, where_k, axis=0)
            chosen_cols = jnp.take(local_bcols, where_k, axis=0)
            picked = select_blocks(chosen, chosen_cols, wanted[:, None, None, :])
            return jnp.einsum("isab,iscbd->icad", left, picked, preferred_element_type=jnp.float32)

        terms = lax.map(one_group, jnp.arange(count // group, dtype=jnp.int32))
        return terms.reshape(count, pattern.shape[1], width, width)

    return partial_term


def per_device(a_blocks, a_cols, b_blocks, b_cols, c_cols):
    own_rows = a_blocks.shape[0]
    local_b = b_blocks[:, 0]
    local_bcols = b_cols[:, 0]
    pattern = c_cols[:, 0]
    per_pattern = pattern.shape[1]
    routed, slab_cols = (
        lax.all_to_all(a_blocks, "blk", split_axis=1, concat_axis=0, tiled=True),
        lax.all_to_all(a_cols, "blk", split_axis=1, concat_axis=0, tiled=True),
    )
    slab = lax.all_gather(routed, "rep", axis=4, tiled=True)
    partial_term = term_maker(slab, slab_cols, local_b, local_bcols, pattern)
    mine = lax.psum_scatter(
        partial_term(jnp.int32(0), own_rows * lax.axis_size("blk")),
        "blk",
        scatter_dimension=0,
        tiled=True,
    )
    width = a_blocks.shape[3]
    return mine.reshape(own_rows, 1, per_pattern, width, width)


def solution(mesh):
    placed = (
        P("blk", None, None, None, "rep"),
        P("blk", None, None),
        P("blk", "rep", None, None, None),
        P("blk", "rep", None),
        P(None, "rep", None),
    )
    return jax.shard_map(
        per_device,
        mesh=mesh,
        in_specs=placed,
        out_specs=P("blk", "rep", None, None, None),
        check_vma=False,
    )
```

profile of v0, /device:TPU:0, one launch (start us, length us, event | category | flops | bytes accessed | tf_op | source)
XLA Modules:
  0.0 355.9 jit_solution(1189941406154972925)
XLA Ops:
  6.5 1.5 copy.32
  8.0 36.0 %all_to_all.33 = bf16[3,8,6,128,32]{3,4,2,0,1:T(8,128)(2,1)S(1)} all-to-all(bf16[3,8,6,128,32]{3,4,2,0,1:T(8,128)(2,1)S(1)} %copy.32), channel_id=1, replica_groups=mesh['blk'=8,'rep'=4] {'blk'}, dimensions={1} | all-to-all | bytes 2359296 | tf_op jit(solution)/shard_map/all_to_all | solution.py:54
  44.0 1.8 copy.33
  45.8 0.6 copy.29
  46.4 3.3 all-to-all-start
  50.0 6.2 %all-to-all-done = s32[3,8,6]{2,0,1:T(4,128)S(1)} async-done(((s32[3,8,6]{2,0,1:T(4,128)}), s32[3,8,6]{2,0,1:T(4,128)S(1)}, u32[]{:S(2)}, u32[]{:S(2)}) %all-to-all-start) | async-done | bytes 608 | tf_op jit(solution)/shard_map/all_to_all | solution.py:55
  56.3 25.8 %all-gather.2.cloned.1.call-done = bf16[24,1,6,128,128]{3,0,2,1,4:T(8,128)(2,1)} async-done(((bf16[24,1,6,128,32]{3,0,2,1,4:T(8,128)(2,1)}), bf16[24,1,6,128,128]{3,0,2,1,4:T(8,128)(2,1)}) %all-gather.2.cloned.1.call-update) | async-done | bytes 4718608 | tf_op jit(solution)/shard_map/all_gather | solution.py:57
  82.1 148.8 %while.10 = (s32[]{:T(128)}, f32[12,2,4,128,128]{4,3,2,1,0:T(8,128)}, s32[12]{0:T(128)S(1)}, s32[24,6]{1,0:T(8,128)S(1)}, s32[112,3]{1,0:T(8,128)S(1)}, /*index=...) while((s32[]{:T(128)}, ...), condition=%wide.region_1.2_spmd, body=%wide.region_0.1_spmd.sunk | while | flops 205849856 | bytes 15211487 | solution.py:41
  82.1 0.6 dynamic_slice.22
  84.3 4.9 %gather_fusion.1 = bf16[12,3,128,128]{3,2,1,0:T(8,128)(2,1)S(1)} fusion(bf16[112,3,128,128]{3,2,1,0:T(8,128)(2,1)} %get-tuple-element.191, s32[1024]{0:T(1024)S(1)} %pad_clamp_fusion.2), kind=kCustom, calls=%fused_computation.1.clone.1 | custom fusion | bytes 2359344 | tf_op jit(solution)/shard_map/while/body/eval_jaxpr/jit(_take)/gather | solution.py:36
  90.2 1.8 constant_dynamic-slice_fusion.5
  92.5 0.9 fusion.23
  93.6 0.8 constant_dynamic-update-slice_fusion.2
  94.5 0.6 dynamic_slice.22
  96.7 4.9 %gather_fusion.1 = bf16[12,3,128,128]{3,2,1,0:T(8,128)(2,1)S(1)} fusion(bf16[112,3,128,128]{3,2,1,0:T(8,128)(2,1)} %get-tuple-element.191, s32[1024]{0:T(1024)S(1)} %pad_clamp_fusion.2), kind=kCustom, calls=%fused_computation.1.clone.1 | custom fusion | bytes 2359344 | tf_op jit(solution)/shard_map/while/body/eval_jaxpr/jit(_take)/gather | solution.py:36
  102.6 1.8 constant_dynamic-slice_fusion.5
  104.9 0.9 fusion.23
  106.0 0.8 constant_dynamic-update-slice_fusion.2
  106.9 0.6 dynamic_slice.22
  109.1 4.9 %gather_fusion.1 = bf16[12,3,128,128]{3,2,1,0:T(8,128)(2,1)S(1)} fusion(bf16[112,3,128,128]{3,2,1,0:T(8,128)(2,1)} %get-tuple-element.191, s32[1024]{0:T(1024)S(1)} %pad_clamp_fusion.2), kind=kCustom, calls=%fused_computation.1.clone.1 | custom fusion | bytes 2359344 | tf_op jit(solution)/shard_map/while/body/eval_jaxpr/jit(_take)/gather | solution.py:36
  115.0 1.8 constant_dynamic-slice_fusion.5
  117.3 0.9 fusion.23
  118.4 0.9 constant_dynamic-update-slice_fusion.2
  119.3 0.6 dynamic_slice.22
  121.5 4.9 %gather_fusion.1 = bf16[12,3,128,128]{3,2,1,0:T(8,128)(2,1)S(1)} fusion(bf16[112,3,128,128]{3,2,1,0:T(8,128)(2,1)} %get-tuple-element.191, s32[1024]{0:T(1024)S(1)} %pad_clamp_fusion.2), kind=kCustom, calls=%fused_computation.1.clone.1 | custom fusion | bytes 2359344 | tf_op jit(solution)/shard_map/while/body/eval_jaxpr/jit(_take)/gather | solution.py:36
  127.4 1.8 constant_dynamic-slice_fusion.5
  129.7 0.9 fusion.23
  130.8 0.9 constant_dynamic-update-slice_fusion.2
  133.9 4.9 %gather_fusion.1 = bf16[12,3,128,128]{3,2,1,0:T(8,128)(2,1)S(1)} fusion(bf16[112,3,128,128]{3,2,1,0:T(8,128)(2,1)} %get-tuple-element.191, s32[1024]{0:T(1024)S(1)} %pad_clamp_fusion.2), kind=kCustom, calls=%fused_computation.1.clone.1 | custom fusion | bytes 2359344 | tf_op jit(solution)/shard_map/while/body/eval_jaxpr/jit(_take)/gather | solution.py:36
  139.8 1.8 constant_dynamic-slice_fusion.5
  142.1 0.9 fusion.23
  143.2 0.9 constant_dynamic-update-slice_fusion.2
  146.3 4.9 %gather_fusion.1 = bf16[12,3,128,128]{3,2,1,0:T(8,128)(2,1)S(1)} fusion(bf16[112,3,128,128]{3,2,1,0:T(8,128)(2,1)} %get-tuple-element.191, s32[1024]{0:T(1024)S(1)} %pad_clamp_fusion.2), kind=kCustom, calls=%fused_computation.1.clone.1 | custom fusion | bytes 2359344 | tf_op jit(solution)/shard_map/while/body/eval_jaxpr/jit(_take)/gather | solution.py:36
  152.2 1.8 constant_dynamic-slice_fusion.5
  154.5 0.9 fusion.23
  155.6 0.9 constant_dynamic-update-slice_fusion.2
  158.7 4.9 %gather_fusion.1 = bf16[12,3,128,128]{3,2,1,0:T(8,128)(2,1)S(1)} fusion(bf16[112,3,128,128]{3,2,1,0:T(8,128)(2,1)} %get-tuple-element.191, s32[1024]{0:T(1024)S(1)} %pad_clamp_fusion.2), kind=kCustom, calls=%fused_computation.1.clone.1 | custom fusion | bytes 2359344 | tf_op jit(solution)/shard_map/while/body/eval_jaxpr/jit(_take)/gather | solution.py:36
  164.6 1.8 constant_dynamic-slice_fusion.5
  166.9 0.9 fusion.23
  168.0 0.9 constant_dynamic-update-slice_fusion.2
  168.9 0.6 dynamic_slice.22
  171.1 4.9 %gather_fusion.1 = bf16[12,3,128,128]{3,2,1,0:T(8,128)(2,1)S(1)} fusion(bf16[112,3,128,128]{3,2,1,0:T(8,128)(2,1)} %get-tuple-element.191, s32[1024]{0:T(1024)S(1)} %pad_clamp_fusion.2), kind=kCustom, calls=%fused_computation.1.clone.1 | custom fusion | bytes 2359344 | tf_op jit(solution)/shard_map/while/body/eval_jaxpr/jit(_take)/gather | solution.py:36
  177.0 1.8 constant_dynamic-slice_fusion.5
  179.3 0.9 fusion.23
  180.4 0.8 constant_dynamic-update-slice_fusion.2
  181.3 0.6 dynamic_slice.22
  183.5 4.9 %gather_fusion.1 = bf16[12,3,128,128]{3,2,1,0:T(8,128)(2,1)S(1)} fusion(bf16[112,3,128,128]{3,2,1,0:T(8,128)(2,1)} %get-tuple-element.191, s32[1024]{0:T(1024)S(1)} %pad_clamp_fusion.2), kind=kCustom, calls=%fused_computation.1.clone.1 | custom fusion | bytes 2359344 | tf_op jit(solution)/shard_map/while/body/eval_jaxpr/jit(_take)/gather | solution.py:36
  189.4 1.8 constant_dynamic-slice_fusion.5
  191.7 0.9 fusion.23
  192.8 0.8 constant_dynamic-update-slice_fusion.2
  193.7 0.6 dynamic_slice.22
  195.8 4.9 %gather_fusion.1 = bf16[12,3,128,128]{3,2,1,0:T(8,128)(2,1)S(1)} fusion(bf16[112,3,128,128]{3,2,1,0:T(8,128)(2,1)} %get-tuple-element.191, s32[1024]{0:T(1024)S(1)} %pad_clamp_fusion.2), kind=kCustom, calls=%fused_computation.1.clone.1 | custom fusion | bytes 2359344 | tf_op jit(solution)/shard_map/while/body/eval_jaxpr/jit(_take)/gather | solution.py:36
  201.8 1.8 constant_dynamic-slice_fusion.5
  204.1 0.9 fusion.23
  205.2 0.8 constant_dynamic-update-slice_fusion.2
  208.2 4.9 %gather_fusion.1 = bf16[12,3,128,128]{3,2,1,0:T(8,128)(2,1)S(1)} fusion(bf16[112,3,128,128]{3,2,1,0:T(8,128)(2,1)} %get-tuple-element.191, s32[1024]{0:T(1024)S(1)} %pad_clamp_fusion.2), kind=kCustom, calls=%fused_computation.1.clone.1 | custom fusion | bytes 2359344 | tf_op jit(solution)/shard_map/while/body/eval_jaxpr/jit(_take)/gather | solution.py:36
  214.1 1.8 constant_dynamic-slice_fusion.5
  216.5 0.9 fusion.23
  217.6 0.9 constant_dynamic-update-slice_fusion.2
  220.7 4.9 %gather_fusion.1 = bf16[12,3,128,128]{3,2,1,0:T(8,128)(2,1)S(1)} fusion(bf16[112,3,128,128]{3,2,1,0:T(8,128)(2,1)} %get-tuple-element.191, s32[1024]{0:T(1024)S(1)} %pad_clamp_fusion.2), kind=kCustom, calls=%fused_computation.1.clone.1 | custom fusion | bytes 2359344 | tf_op jit(solution)/shard_map/while/body/eval_jaxpr/jit(_take)/gather | solution.py:36
  226.6 1.8 constant_dynamic-slice_fusion.5
  228.9 0.9 fusion.23
  230.0 0.8 constant_dynamic-update-slice_fusion.2
  230.9 118.2 %reduce-scatter.2.cloned.1.call-done = f32[3,4,128,128]{3,2,1,0:T(8,128)} async-done(((f32[24,4,128,128]{3,2,1,0:T(8,128)}), f32[3,4,128,128]{3,2,1,0:T(8,128)}) %reduce-scatter.2.cloned.1.call-update) | async-done | bytes 786448 | tf_op jit(solution)/shard_map/reduce_scatter | solution.py:59
  (224 shorter events, 34.2 us)
Async XLA Ops:
  6.5 75.6 %all-gather.2.cloned.1.call-start = ((), (), s32[]{:S(2)}) async-start(), calls=%async_computation.3 | async-start | bytes 5898240 | tf_op jit(solution)/shard_map/all_gather | solution.py:57
  44.0 1.8 copy-start
  44.0 5.8 %copy-start.2 = (s32[112,1,3]{0,1,2:T(1,128)S(1)}, s32[112,1,3]{0,1,2:T(1,128)}, u32[]{:S(2)}) copy-start(s32[112,1,3]{0,1,2:T(1,128)} %param.10) | copy-start | bytes 4036
  44.0 5.9 %copy-start.1 = (s32[24,1,4]{0,2,1:T(4,128)S(1)}, s32[24,1,4]{0,2,1:T(4,128)}, u32[]{:S(2)}) copy-start(s32[24,1,4]{0,2,1:T(4,128)} %param.11) | copy-start | bytes 1156
  46.4 9.9 %all-to-all-start = ((s32[3,8,6]{2,0,1:T(4,128)}), s32[3,8,6]{2,0,1:T(4,128)S(1)}, u32[]{:S(2)}, u32[]{:S(2)}) async-start(s32[3,8,6]{2,0,1:T(4,128)} %copy.29), calls=%async_computation | async-start | bytes 32768 | tf_op jit(solution)/shard_map/all_to_all | solution.py:55
  49.8 299.3 %reduce-scatter.2.cloned.1.call-start = ((), (), s32[]{:S(2)}) async-start(), calls=%async_computation.4 | async-start | bytes 7077888 | tf_op jit(solution)/shard_map/reduce_scatter | solution.py:59
Sparse Core Ops, SparseCore 0:
  45.9 36.1 all-gather.1
  231.0 118.0 reduce-scatter.1
where the time goes:
time: 357 us; the launch traced here: 356 us
  waiting for transfers between devices  150 us (42%)
  local copies, waits for them, and re-layouts  130 us (36%)
  blocking collectives  36 us (10%)
  between operations  13.4 us (4%)
  matrix products  10.9 us (3%)
  loops' own time  8.92 us (2%)
    reduce_scatter x1, waiting for transfers between devices, per_device(): lax.psum_scatter(partial_term(jnp.int32(0), own_rows * lax.axis_size('blk...  118 us
    gather x12, local copies, waits for them, and re-layouts, one_group(): chosen = jnp.take(local_b, where_k, axis=0)  58.8 us
    all_to_all x1, blocking collectives, per_device(): lax.all_to_all(a_blocks, 'blk', split_axis=1, concat_axis=0, tiled=True)  36 us
    dynamic_slice x24, local copies, waits for them, and re-layouts, one_group(): left = lax.dynamic_slice_in_dim(slab, first, group, 0)  27.7 us
    all_gather x1, waiting for transfers between devices, per_device(): slab = lax.all_gather(routed, 'rep', axis=4, tiled=True)  25.8 us
    dynamic_update_slice x24, local copies, waits for them, and re-layouts, partial_term(): terms = lax.map(one_group, jnp.arange(count // group, dtype=jnp.int32))  12.6 us
    dot_general x12, matrix products, one_group(): jnp.einsum('isab,iscbd->icad', left, picked, preferred_element_type=jnp.f...  10.9 us
    broadcast_in_dim x60, local copies, waits for them, and re-layouts, select_blocks(): jnp.where(hits[..., slot_t, :, None, None], chosen[..., slot_t, None, :,...  9.59 us
  transfers between devices with their start and end apart: 3, of which 3 were waited for; matrix products, arithmetic and copies ran while one was open for 0% of the time, Pallas kernels for 0%

commit v1 on v0

--- a/solution.py
+++ b/solution.py
@@ -1,8 +1,24 @@
+import functools
 import math
 import jax
 import jax.numpy as jnp
 from jax import lax
 from jax.sharding import PartitionSpec as P
+
+
+def match_the_goods(local_x, peer_axis):
+    w1, z1 = (lax.psum(1, peer_axis), lax.axis_index(peer_axis))
+    fresh, z = (local_x, 1)
+    while z < w1:
+        then = lax.ppermute(fresh, peer_axis, perm=[(ii, ii ^ z) for ii in range(w1)])
+        local_part = jnp.concatenate([fresh, then], 4)
+        t_next = jnp.concatenate([then, fresh], 4)
+        fresh = jnp.where(z1 & z == 0, local_part, t_next)
+        z = 2 * z
+    return fresh
+
+
+_choose_positions = functools.partial(match_the_goods, peer_axis="rep")
 
 
 def select_blocks(chosen, chosen_cols, wanted):
@@ -54,7 +70,7 @@
         lax.all_to_all(a_blocks, "blk", split_axis=1, concat_axis=0, tiled=True),
         lax.all_to_all(a_cols, "blk", split_axis=1, concat_axis=0, tiled=True),
     )
-    slab = lax.all_gather(routed, "rep", axis=4, tiled=True)
+    slab = _choose_positions(routed)
     partial_term = term_maker(slab, slab_cols, local_b, local_bcols, pattern)
     mine = lax.psum_scatter(
         partial_term(jnp.int32(0), own_rows * lax.axis_size("blk")),

time: 357 us -> 363 us (1.017)
  local copies, waits for them, and re-layouts: 130 us -> 99.8 us
  waiting for transfers between devices: 150 us -> 167 us
  other arithmetic: 3.44 us -> 12.7 us
  matrix products: 10.9 us -> 19.5 us
    ppermute x0 -> x2, waiting for transfers between devices: none -> 43.7 us  [match_the_goods(): lax.ppermute(fresh, peer_axis, perm=[(ii, ii ^ z) for ii in range(w1)])]
    dynamic_slice x24 -> x0, local copies, waits for them, and re-layouts: 27.7 us -> none  [one_group(): left = lax.dynamic_slice_in_dim(slab, first, group, 0)]
    all_gather x1 -> x0, waiting for transfers between devices: 25.8 us -> none  [per_device(): slab = lax.all_gather(routed, 'rep', axis=4, tiled=True)]
    select_n x0 -> x3, other arithmetic: none -> 9.24 us  [match_the_goods(): fresh = jnp.where(z1 & z == 0, local_part, t_next)]
    dot_general x12, matrix products: 10.9 us -> 19.5 us  [one_group(): jnp.einsum('isab,iscbd->icad', left, picked, preferred_element_type=jnp.f...]
  transfers between devices with their start and end apart: 3 -> 4, of which waited for: 3 -> 4; matrix products, arithmetic and copies ran while one was open for 0% -> 0% of each run, Pallas kernels for 0% -> 0%
where the time goes in v1:
time: 363 us; the launch traced here: 362 us
  waiting for transfers between devices  167 us (46%)
  local copies, waits for them, and re-layouts  99.8 us (27%)
  blocking collectives  36 us (10%)
  matrix products  19.5 us (5%)
  between operations  13.5 us (4%)
  other arithmetic  12.7 us (3%)
  loops' own time  8.72 us (2%)
  starting transfers between devices  4.9 us (1%)
    reduce_scatter x1, waiting for transfers between devices, per_device(): lax.psum_scatter(partial_term(jnp.int32(0), own_rows * lax.axis_size('blk...  117 us
    gather x12, local copies, waits for them, and re-layouts, one_group(): chosen = jnp.take(local_b, where_k, axis=0)  58.8 us
    ppermute x2, waiting for transfers between devices, match_the_goods(): lax.ppermute(fresh, peer_axis, perm=[(ii, ii ^ z) for ii in range(w1)])  43.7 us
    all_to_all x1, blocking collectives, per_device(): lax.all_to_all(a_blocks, 'blk', split_axis=1, concat_axis=0, tiled=True)  36 us
    dot_general x12, matrix products, one_group(): jnp.einsum('isab,iscbd->icad', left, picked, preferred_element_type=jnp.f...  19.5 us
    dynamic_update_slice x24, local copies, waits for them, and re-layouts, partial_term(): terms = lax.map(one_group, jnp.arange(count // group, dtype=jnp.int32))  12.5 us
    broadcast_in_dim x60, local copies, waits for them, and re-layouts, select_blocks(): jnp.where(hits[..., slot_t, :, None, None], chosen[..., slot_t, None, :,...  9.32 us
    select_n x3, other arithmetic, match_the_goods(): fresh = jnp.where(z1 & z == 0, local_part, t_next)  9.24 us
  transfers between devices with their start and end apart: 4, of which 4 were waited for; matrix products, arithmetic and copies ran while one was open for 0% of the time, Pallas kernels for 0%

profile of v1, /device:TPU:0, one launch (start us, length us, event | category | flops | bytes accessed | tf_op | source)
XLA Modules:
  0.0 361.9 jit_solution(17109297668415567814)
XLA Ops:
  6.5 1.5 copy.34
  8.0 36.0 %all_to_all.33 = bf16[3,8,6,128,32]{3,4,2,0,1:T(8,128)(2,1)S(1)} all-to-all(bf16[3,8,6,128,32]{3,4,2,0,1:T(8,128)(2,1)S(1)} %copy.34), channel_id=1, replica_groups=mesh['blk'=8,'rep'=4] {'blk'}, dimensions={1} | all-to-all | bytes 2359296 | tf_op jit(solution)/shard_map/all_to_all | solution.py:70
  44.0 2.8 collective-permute-done
  46.8 1.9 maximum_select_fusion.2
  48.8 1.5 collective-permute-start.1
  50.3 0.6 copy.31
  50.9 3.3 all-to-all-start
  54.5 6.2 %all-to-all-done = s32[3,8,6]{2,0,1:T(4,128)S(1)} async-done(((s32[3,8,6]{2,0,1:T(4,128)}), s32[3,8,6]{2,0,1:T(4,128)S(1)}, u32[]{:S(2)}, u32[]{:S(2)}) %all-to-all-start) | async-done | bytes 608 | tf_op jit(solution)/shard_map/all_to_all | solution.py:71
  60.8 0.7 maximum_select_fusion.1
  61.5 40.9 %collective-permute-done.1 = bf16[24,1,6,128,64]{3,4,2,1,0:T(8,128)(2,1)} collective-permute-done((bf16[24,1,6,128,64]{3,4,2,1,0:T(8,128)(2,1)}, bf16[24,1,6,128,64]{3,4,2,1,0:T(8,128)(2,1)}, u32[]{:S(2)}, u32[]{:S(2)}) %collective-permute-start.1) | collective-permute-done | bytes 2359328 | tf_op jit(solution)/shard_map/ppermute | solution.py:13
  102.4 6.6 %maximum_select_fusion = bf16[24,6,128,128]{2,3,1,0:T(8,128)(2,1)} fusion(bf16[24,6,128,64]{2,3,1,0:T(8,128)(2,1)} %bitcast.30, bf16[24,6,128,64]{2,3,1,0:T(8,128)(2,1)S(1)} %maximum_select_fusion.1, pred[]{:T(512)S(6)} %eq.19), kind=kLoop, calls=%fused_computation.34 | loop fusion | flops 21233664 | bytes 9437185 | tf_op jit(solution)/shard_map/jit(_where)/select_n | solution.py:16
  109.0 129.2 %while.10 = (s32[]{:T(128)}, f32[12,2,4,128,128]{4,3,2,1,0:T(8,128)}, s32[12]{0:T(128)S(1)}, s32[24,6]{1,0:T(8,128)S(1)}, s32[112,3]{1,0:T(8,128)S(1)}, /*index=...) while((s32[]{:T(128)}, ...), condition=%wide.region_1.2_spmd, body=%wide.region_0.1_spmd.sunk | while | flops 205849856 | bytes 13638623 | solution.py:57
  109.0 0.6 dynamic_slice.25
  110.3 0.6 gather_fusion
  111.2 4.9 %gather_fusion.1 = bf16[12,3,128,128]{3,2,1,0:T(8,128)(2,1)S(1)} fusion(bf16[112,3,128,128]{3,2,1,0:T(8,128)(2,1)} %get-tuple-element.191, s32[1024]{0:T(1024)S(1)} %pad_clamp_fusion.2), kind=kCustom, calls=%fused_computation.1.clone.1 | custom fusion | bytes 2359344 | tf_op jit(solution)/shard_map/while/body/eval_jaxpr/jit(_take)/gather | solution.py:52
  117.1 1.6 fusion.25
  118.9 0.8 constant_dynamic-update-slice_fusion.2
  119.7 0.6 dynamic_slice.25
  121.1 0.6 gather_fusion
  121.9 4.9 %gather_fusion.1 = bf16[12,3,128,128]{3,2,1,0:T(8,128)(2,1)S(1)} fusion(bf16[112,3,128,128]{3,2,1,0:T(8,128)(2,1)} %get-tuple-element.191, s32[1024]{0:T(1024)S(1)} %pad_clamp_fusion.2), kind=kCustom, calls=%fused_computation.1.clone.1 | custom fusion | bytes 2359344 | tf_op jit(solution)/shard_map/while/body/eval_jaxpr/jit(_take)/gather | solution.py:52
  127.8 1.6 fusion.25
  129.6 0.8 constant_dynamic-update-slice_fusion.2
  130.5 0.6 dynamic_slice.25
  132.7 4.9 %gather_fusion.1 = bf16[12,3,128,128]{3,2,1,0:T(8,128)(2,1)S(1)} fusion(bf16[112,3,128,128]{3,2,1,0:T(8,128)(2,1)} %get-tuple-element.191, s32[1024]{0:T(1024)S(1)} %pad_clamp_fusion.2), kind=kCustom, calls=%fused_computation.1.clone.1 | custom fusion | bytes 2359344 | tf_op jit(solution)/shard_map/while/body/eval_jaxpr/jit(_take)/gather | solution.py:52
  138.6 1.6 fusion.25
  140.4 0.9 constant_dynamic-update-slice_fusion.2
  141.3 0.6 dynamic_slice.25
  142.6 0.6 gather_fusion
  143.4 4.9 %gather_fusion.1 = bf16[12,3,128,128]{3,2,1,0:T(8,128)(2,1)S(1)} fusion(bf16[112,3,128,128]{3,2,1,0:T(8,128)(2,1)} %get-tuple-element.191, s32[1024]{0:T(1024)S(1)} %pad_clamp_fusion.2), kind=kCustom, calls=%fused_computation.1.clone.1 | custom fusion | bytes 2359344 | tf_op jit(solution)/shard_map/while/body/eval_jaxpr/jit(_take)/gather | solution.py:52
  149.3 1.6 fusion.25
  151.2 0.8 constant_dynamic-update-slice_fusion.2
  152.0 0.6 dynamic_slice.25
  154.2 4.9 %gather_fusion.1 = bf16[12,3,128,128]{3,2,1,0:T(8,128)(2,1)S(1)} fusion(bf16[112,3,128,128]{3,2,1,0:T(8,128)(2,1)} %get-tuple-element.191, s32[1024]{0:T(1024)S(1)} %pad_clamp_fusion.2), kind=kCustom, calls=%fused_computation.1.clone.1 | custom fusion | bytes 2359344 | tf_op jit(solution)/shard_map/while/body/eval_jaxpr/jit(_take)/gather | solution.py:52
  160.1 1.6 fusion.25
  161.9 0.8 constant_dynamic-update-slice_fusion.2
  162.8 0.6 dynamic_slice.25
  165.0 4.9 %gather_fusion.1 = bf16[12,3,128,128]{3,2,1,0:T(8,128)(2,1)S(1)} fusion(bf16[112,3,128,128]{3,2,1,0:T(8,128)(2,1)} %get-tuple-element.191, s32[1024]{0:T(1024)S(1)} %pad_clamp_fusion.2), kind=kCustom, calls=%fused_computation.1.clone.1 | custom fusion | bytes 2359344 | tf_op jit(solution)/shard_map/while/body/eval_jaxpr/jit(_take)/gather | solution.py:52
  170.9 1.6 fusion.25
  172.7 0.8 constant_dynamic-update-slice_fusion.2
  173.5 0.6 dynamic_slice.25
  175.7 4.9 %gather_fusion.1 = bf16[12,3,128,128]{3,2,1,0:T(8,128)(2,1)S(1)} fusion(bf16[112,3,128,128]{3,2,1,0:T(8,128)(2,1)} %get-tuple-element.191, s32[1024]{0:T(1024)S(1)} %pad_clamp_fusion.2), kind=kCustom, calls=%fused_computation.1.clone.1 | custom fusion | bytes 2359344 | tf_op jit(solution)/shard_map/while/body/eval_jaxpr/jit(_take)/gather | solution.py:52
  181.6 1.6 fusion.25
  183.5 0.9 constant_dynamic-update-slice_fusion.2
  184.3 0.6 dynamic_slice.25
  186.5 4.9 %gather_fusion.1 = bf16[12,3,128,128]{3,2,1,0:T(8,128)(2,1)S(1)} fusion(bf16[112,3,128,128]{3,2,1,0:T(8,128)(2,1)} %get-tuple-element.191, s32[1024]{0:T(1024)S(1)} %pad_clamp_fusion.2), kind=kCustom, calls=%fused_computation.1.clone.1 | custom fusion | bytes 2359344 | tf_op jit(solution)/shard_map/while/body/eval_jaxpr/jit(_take)/gather | solution.py:52
  192.4 1.6 fusion.25
  194.2 0.8 constant_dynamic-update-slice_fusion.2
  195.1 0.6 dynamic_slice.25
  197.3 4.9 %gather_fusion.1 = bf16[12,3,128,128]{3,2,1,0:T(8,128)(2,1)S(1)} fusion(bf16[112,3,128,128]{3,2,1,0:T(8,128)(2,1)} %get-tuple-element.191, s32[1024]{0:T(1024)S(1)} %pad_clamp_fusion.2), kind=kCustom, calls=%fused_computation.1.clone.1 | custom fusion | bytes 2359344 | tf_op jit(solution)/shard_map/while/body/eval_jaxpr/jit(_take)/gather | solution.py:52
  203.2 1.6 fusion.25
  205.0 0.8 constant_dynamic-update-slice_fusion.2
  205.8 0.6 dynamic_slice.25
  208.0 4.9 %gather_fusion.1 = bf16[12,3,128,128]{3,2,1,0:T(8,128)(2,1)S(1)} fusion(bf16[112,3,128,128]{3,2,1,0:T(8,128)(2,1)} %get-tuple-element.191, s32[1024]{0:T(1024)S(1)} %pad_clamp_fusion.2), kind=kCustom, calls=%fused_computation.1.clone.1 | custom fusion | bytes 2359344 | tf_op jit(solution)/shard_map/while/body/eval_jaxpr/jit(_take)/gather | solution.py:52
  213.9 1.6 fusion.25
  215.8 0.8 constant_dynamic-update-slice_fusion.2
  216.6 0.6 dynamic_slice.25
  218.8 4.9 %gather_fusion.1 = bf16[12,3,128,128]{3,2,1,0:T(8,128)(2,1)S(1)} fusion(bf16[112,3,128,128]{3,2,1,0:T(8,128)(2,1)} %get-tuple-element.191, s32[1024]{0:T(1024)S(1)} %pad_clamp_fusion.2), kind=kCustom, calls=%fused_computation.1.clone.1 | custom fusion | bytes 2359344 | tf_op jit(solution)/shard_map/while/body/eval_jaxpr/jit(_take)/gather | solution.py:52
  224.7 1.6 fusion.25
  226.5 0.9 constant_dynamic-update-slice_fusion.2
  227.4 0.6 dynamic_slice.25
  229.6 4.9 %gather_fusion.1 = bf16[12,3,128,128]{3,2,1,0:T(8,128)(2,1)S(1)} fusion(bf16[112,3,128,128]{3,2,1,0:T(8,128)(2,1)} %get-tuple-element.191, s32[1024]{0:T(1024)S(1)} %pad_clamp_fusion.2), kind=kCustom, calls=%fused_computation.1.clone.1 | custom fusion | bytes 2359344 | tf_op jit(solution)/shard_map/while/body/eval_jaxpr/jit(_take)/gather | solution.py:52
  235.5 1.6 fusion.25
  237.3 0.8 constant_dynamic-update-slice_fusion.2
  238.2 116.9 %reduce-scatter.2.cloned.1.call-done = f32[3,4,128,128]{3,2,1,0:T(8,128)} async-done(((f32[24,4,128,128]{3,2,1,0:T(8,128)}), f32[3,4,128,128]{3,2,1,0:T(8,128)}) %reduce-scatter.2.cloned.1.call-update) | async-done | bytes 786448 | tf_op jit(solution)/shard_map/reduce_scatter | solution.py:75
  (203 shorter events, 23.5 us)
Async XLA Ops:
  44.0 2.8 collective-permute-start
  44.0 6.3 %copy-start = (s32[3,8,6]{2,1,0:T(8,128)S(1)}, s32[3,8,6]{2,1,0:T(8,128)}, u32[]{:S(2)}) copy-start(s32[3,8,6]{2,1,0:T(8,128)} %param.8) | copy-start | bytes 1732
  44.0 10.3 %copy-start.2 = (s32[112,1,3]{0,1,2:T(1,128)S(1)}, s32[112,1,3]{0,1,2:T(1,128)}, u32[]{:S(2)}) copy-start(s32[112,1,3]{0,1,2:T(1,128)} %param.10) | copy-start | bytes 4036
  44.0 10.4 %copy-start.1 = (s32[24,1,4]{0,2,1:T(4,128)S(1)}, s32[24,1,4]{0,2,1:T(4,128)}, u32[]{:S(2)}) copy-start(s32[24,1,4]{0,2,1:T(4,128)} %param.11) | copy-start | bytes 1156
  48.8 53.6 %collective-permute-start.1 = (bf16[24,1,6,128,64]{3,4,2,1,0:T(8,128)(2,1)}, bf16[24,1,6,128,64]{3,4,2,1,0:T(8,128)(2,1)}, u32[]{:S(2)}, u32[]{:S(2)}) collective-permute-start(bf16[24,1,6,128,64]{3,4,2,1,0:T(8,128)(2,1)} %maximum_select_fusion.2), channel_id=1, source_target_pairs={{0,2},{1,3},{2,0},{3,1},{4,6},{5,7},{6,4},{7,5},{8,10},{9,11},{10,... | collective-permute-start | bytes 7077896 | tf_op jit(solution)/shard_map/ppermute | solution.py:13
  50.9 9.9 %all-to-all-start = ((s32[3,8,6]{2,0,1:T(4,128)}), s32[3,8,6]{2,0,1:T(4,128)S(1)}, u32[]{:S(2)}, u32[]{:S(2)}) async-start(s32[3,8,6]{2,0,1:T(4,128)} %copy.31), calls=%async_computation | async-start | bytes 32768 | tf_op jit(solution)/shard_map/all_to_all | solution.py:71
  54.3 300.8 %reduce-scatter.2.cloned.1.call-start = ((), (), s32[]{:S(2)}) async-start(), calls=%async_computation.3 | async-start | bytes 7077888 | tf_op jit(solution)/shard_map/reduce_scatter | solution.py:75
Sparse Core Ops, SparseCore 0:
  238.3 116.7 reduce-scatter.1
